TPU v7x, 32 devices: a whole 2x2x4 slice. The times are simulated.
32 devices in a mesh: view: 4 (over x, core), samp: 8 (over z, y).
Axes of the slice: x: 2, y: 2, z: 4, core: 2. Of those that a mesh axis runs over, the one named last changes fastest.
Arguments:
- view_data: bfloat16 [8, 4096, 2048], P('view', 'samp'), may hold values from -10 to 10
- init_coeffs: float32 [8, 2048, 128], P('view'), may hold values from -0.125 to 0.125
Outputs:
- shared_scores: float32 [4096, 128], P('samp')
- final_coeffs: float32 [8, 2048, 128], P('view', 'samp')
All inputs are finite; a program needn't handle non-finite values.
Results may differ from a plain program's by a relative error of at most 0.005.
Values may be sent and summed in bfloat16 or wider, within the bound.
No kernel may reach another device: no remote copies, remote signals or barrier semaphores. Data moves between devices by JAX's collectives and lax.ppermute only.
A program may use at most 128 MiB of HBM per device.

v0:
```python
import jax
import jax.numpy as jnp
from jax import lax
from jax.sharding import PartitionSpec as P

OUTER = 2
INNER = 2
NS_ITERS = 12
HIGH = lax.Precision.HIGHEST
ridge_weight = 0.1
step_size = 0.5


def newton_inverse(gram):
    size_k = gram.shape[0]
    eye_mat = jnp.eye(size_k, dtype=jnp.float32)
    shrunk = gram + jnp.trace(gram) / size_k * eye_mat
    scale = jnp.sqrt(jnp.sum(shrunk * shrunk))
    approx = shrunk / scale
    inverse = eye_mat
    for turn in range(NS_ITERS):
        factor = 0.5 * (3.0 * eye_mat - jnp.dot(inverse, approx, precision=HIGH))
        approx = jnp.dot(approx, factor, precision=HIGH)
        inverse = jnp.dot(factor, inverse, precision=HIGH)
    return (inverse, scale)


def make_scores(view_data, coeffs_low, total):
    local_sum = jnp.zeros((view_data.shape[1], coeffs_low.shape[2]), jnp.float32)
    for member in range(view_data.shape[0]):
        local_sum = local_sum + jnp.dot(
            view_data[member], coeffs_low[member], preferred_element_type=jnp.float32
        )
    summed = lax.psum(local_sum, "view")
    gram = lax.psum(jnp.dot(summed.T, summed, precision=HIGH), "samp")
    inverse, scale = newton_inverse(gram)
    return jnp.dot(summed, inverse, precision=HIGH) * jnp.sqrt(total / scale)


def grad_term(samples, weights_low, scores):
    resid = (jnp.dot(samples, weights_low, preferred_element_type=jnp.float32) - scores).astype(
        jnp.bfloat16
    )
    return lax.dot_general(
        samples, resid, (((0,), (0,)), ((), ())), preferred_element_type=jnp.float32
    )


def body(view_data, init_coeffs):
    total = view_data.shape[1] * lax.axis_size("samp")
    row_count = init_coeffs.shape[1] // lax.axis_size("samp")
    row_start = lax.axis_index("samp") * row_count
    own_coeffs = lax.dynamic_slice_in_dim(init_coeffs, row_start, row_count, 1)
    coeffs_low = init_coeffs.astype(jnp.bfloat16)
    scores = make_scores(view_data, coeffs_low, total)
    for outer_step in range(OUTER):
        for inner_step in range(INNER):
            terms = jnp.stack(
                [
                    grad_term(view_data[member], coeffs_low[member], scores)
                    for member in range(view_data.shape[0])
                ]
            )
            summed_grad = lax.psum_scatter(terms, "samp", scatter_dimension=1, tiled=True)
            own_coeffs = own_coeffs - step_size * (summed_grad / total + ridge_weight * own_coeffs)
            coeffs_low = lax.all_gather(own_coeffs.astype(jnp.bfloat16), "samp", axis=1, tiled=True)
        scores = make_scores(view_data, coeffs_low, total)
    return (scores, own_coeffs)


def solution(mesh):
    in_specs = (P("view", "samp", None), P("view", None, None))
    out_specs = (P("samp", None), P("view", "samp", None))
    return jax.shard_map(body, mesh=mesh, in_specs=in_specs, out_specs=out_specs, check_vma=False)
```

profile of v0, /device:TPU:0, one launch (start us, length us, event | category | flops | bytes accessed | tf_op | source)
XLA Modules:
  0.0 856.1 jit_solution(11644975215844309981)
XLA Ops:
  7.2 1.9 convert_element_type.42
  9.1 2.3 fusion.12
  11.4 1.4 fusion.163
  12.9 35.1 %all-reduce.7.cloned.1.call-done = f32[512,128]{1,0:T(8,128)} async-done(((f32[512,128]{1,0:T(8,128)}), f32[512,128]{1,0:T(8,128)}) %all-reduce.7.cloned.1.call-update) | async-done | bytes 262160 | tf_op jit(solution)/shard_map/psum | solution.py:34
  48.0 2.2 fusion.165
  50.4 70.9 %all-reduce.9.cloned.1.call-done = f32[128,128]{1,0:T(8,128)} async-done(((f32[128,128]{1,0:T(8,128)}), f32[128,128]{1,0:T(8,128)}) %all-reduce.9.cloned.1.call-update) | async-done | bytes 65552 | tf_op jit(solution)/shard_map/psum | solution.py:35
  121.3 1.5 select_reduce_fusion.2
  123.4 1.5 multiply_reduce_fusion.2
  125.6 1.0 fusion.119
  126.8 1.1 fusion.152
  127.9 0.2 fusion.118
  129.8 0.2 fusion.115
  134.8 0.4 convolution_multiply_fusion.2
  135.1 2.3 convolution_bitcast_fusion.6
  137.6 0.5 convolution_bitcast_fusion.7
  138.0 1.5 pad_maximum_fusion
  139.6 1.0 constant_dynamic-slice_fusion
  140.7 67.8 %reduce-scatter.5.cloned.1.call-done = f32[2,256,128]{1,2,0:T(8,128)} async-done(((f32[2,2048,128]{1,2,0:T(8,128)}), f32[2,256,128]{1,2,0:T(8,128)}) %reduce-scatter.5.cloned.1.call-update) | async-done | bytes 262160 | tf_op jit(solution)/shard_map/reduce_scatter | solution.py:64
  208.5 1.7 fusion.144
  210.3 39.2 %all-gather.5.cloned.1.call-done = bf16[2,2048,128]{1,2,0:T(8,128)(2,1)} async-done(((bf16[2,256,128]{1,2,0:T(8,128)(2,1)}), bf16[2,2048,128]{1,2,0:T(8,128)(2,1)}) %all-gather.5.cloned.1.call-update) | async-done | bytes 1048592 | tf_op jit(solution)/shard_map/all_gather | solution.py:66
  249.5 4.0 convolution_bitcast_fusion.4
  253.4 4.0 convolution_bitcast_fusion.5
  257.4 1.5 pad_maximum_fusion.1
  259.0 68.0 %reduce-scatter.7.cloned.1.call-done = f32[2,256,128]{1,2,0:T(8,128)} async-done(((f32[2,2048,128]{1,2,0:T(8,128)}), f32[2,256,128]{1,2,0:T(8,128)}) %reduce-scatter.7.cloned.1.call-update) | async-done | bytes 262160 | tf_op jit(solution)/shard_map/reduce_scatter | solution.py:64
  327.0 1.7 fusion.162
  328.7 39.1 %all-gather.7.cloned.1.call-done = bf16[2,2048,128]{1,2,0:T(8,128)(2,1)} async-done(((bf16[2,256,128]{1,2,0:T(8,128)(2,1)}), bf16[2,2048,128]{1,2,0:T(8,128)(2,1)}) %all-gather.7.cloned.1.call-update) | async-done | bytes 1048592 | tf_op jit(solution)/shard_map/all_gather | solution.py:66
  367.9 2.7 fusion.55
  370.6 3.1 fusion.164
  373.7 0.2 all-reduce.13.cloned.1.call-start
  374.0 31.2 %all-reduce.11.cloned.1.call-done = f32[512,128]{0,1:T(8,128)} async-done(((f32[512,128]{0,1:T(8,128)}), f32[512,128]{0,1:T(8,128)}) %all-reduce.11.cloned.1.call-update) | async-done | bytes 262160 | tf_op jit(solution)/shard_map/psum | solution.py:34
  405.2 2.0 fusion.187
  407.3 71.1 %all-reduce.13.cloned.1.call-done = f32[128,128]{1,0:T(8,128)} async-done(((f32[128,128]{1,0:T(8,128)}), f32[128,128]{1,0:T(8,128)}) %all-reduce.13.cloned.1.call-update) | async-done | bytes 65552 | tf_op jit(solution)/shard_map/psum | solution.py:35
  478.4 1.5 select_reduce_fusion.1
  480.6 1.5 multiply_reduce_fusion.1
  482.8 1.0 fusion.107
  484.0 1.1 fusion.149
  485.0 0.2 fusion.106
  487.6 0.2 fusion.102
  490.8 0.2 fusion.97
  491.9 0.4 convolution_multiply_fusion.1
  492.3 2.3 convolution_bitcast_fusion.2
  494.7 0.4 convolution_bitcast_fusion.3
  495.2 1.5 pad_maximum_fusion.2
  496.7 69.1 %reduce-scatter.9.cloned.1.call-done = f32[2,256,128]{1,2,0:T(8,128)} async-done(((f32[2,2048,128]{1,2,0:T(8,128)}), f32[2,256,128]{1,2,0:T(8,128)}) %reduce-scatter.9.cloned.1.call-update) | async-done | bytes 262160 | tf_op jit(solution)/shard_map/reduce_scatter | solution.py:64
  565.8 1.7 fusion.145
  567.5 39.2 %all-gather.9.cloned.1.call-done = bf16[2,2048,128]{1,2,0:T(8,128)(2,1)} async-done(((bf16[2,256,128]{1,2,0:T(8,128)(2,1)}), bf16[2,2048,128]{1,2,0:T(8,128)(2,1)}) %all-gather.9.cloned.1.call-update) | async-done | bytes 1048592 | tf_op jit(solution)/shard_map/all_gather | solution.py:66
  606.7 3.6 convolution_bitcast_fusion
  610.3 3.6 convolution_bitcast_fusion.1
  613.9 1.5 pad_maximum_fusion.3
  615.5 68.0 %reduce-scatter.11.cloned.1.call-done = f32[2,256,128]{1,2,0:T(8,128)} async-done(((f32[2,2048,128]{1,2,0:T(8,128)}), f32[2,256,128]{1,2,0:T(8,128)}) %reduce-scatter.11.cloned.1.call-update) | async-done | bytes 262160 | tf_op jit(solution)/shard_map/reduce_scatter | solution.py:64
  683.5 1.7 fusion.161
  685.3 39.1 %all-gather.11.cloned.1.call-done = bf16[2,2048,128]{1,2,0:T(8,128)(2,1)} async-done(((bf16[2,256,128]{1,2,0:T(8,128)(2,1)}), bf16[2,2048,128]{1,2,0:T(8,128)(2,1)}) %all-gather.11.cloned.1.call-update) | async-done | bytes 1048592 | tf_op jit(solution)/shard_map/all_gather | solution.py:66
  724.4 2.7 fusion
  727.1 3.1 fusion.46
  730.3 0.3 all-reduce.17.cloned.1.call-start
  730.5 31.2 %all-reduce.15.cloned.1.call-done = f32[512,128]{0,1:T(8,128)} async-done(((f32[512,128]{0,1:T(8,128)}), f32[512,128]{0,1:T(8,128)}) %all-reduce.15.cloned.1.call-update) | async-done | bytes 262160 | tf_op jit(solution)/shard_map/psum | solution.py:34
  761.7 2.0 fusion.209
  763.8 0.8 copy.6
  764.6 70.2 %all-reduce.17.cloned.1.call-done = f32[128,128]{1,0:T(8,128)} async-done(((f32[128,128]{1,0:T(8,128)}), f32[128,128]{1,0:T(8,128)}) %all-reduce.17.cloned.1.call-update) | async-done | bytes 65552 | tf_op jit(solution)/shard_map/psum | solution.py:35
  834.8 1.5 select_reduce_fusion
  837.0 1.5 multiply_reduce_fusion
  839.2 1.0 fusion.95
  840.4 1.1 fusion.146
  848.3 1.3 convolution_multiply_fusion
  (141 shorter events, 20.3 us)
Async XLA Ops:
  7.2 40.9 %all-reduce.7.cloned.1.call-start = ((), (), s32[]{:S(2)}) async-start(), calls=%async_computation.4 | async-start | bytes 524288 | tf_op jit(solution)/shard_map/psum | solution.py:34
  7.2 4.2 copy-start
  12.9 108.4 %all-reduce.9.cloned.1.call-start = ((), (), s32[]{:S(2)}) async-start(), calls=%async_computation.5 | async-start | bytes 131072 | tf_op jit(solution)/shard_map/psum | solution.py:35
  50.3 158.2 %reduce-scatter.5.cloned.1.call-start = ((), (), s32[]{:S(2)}) async-start(), calls=%async_computation.6 | async-start | bytes 2359296 | tf_op jit(solution)/shard_map/reduce_scatter | solution.py:64
  130.2 4.5 copy-start.4
  134.7 2.8 copy-start.1
  139.6 109.9 %all-gather.5.cloned.1.call-start = ((), (), s32[]{:S(2)}) async-start(), calls=%async_computation.7 | async-start | bytes 1179648 | tf_op jit(solution)/shard_map/all_gather | solution.py:66
  210.2 116.8 %reduce-scatter.7.cloned.1.call-start = ((), (), s32[]{:S(2)}) async-start(), calls=%async_computation.8 | async-start | bytes 2359296 | tf_op jit(solution)/shard_map/reduce_scatter | solution.py:64
  258.9 68.1 %copy-start.6 = (f32[2,256,128]{1,2,0:T(8,128)S(1)}, f32[2,256,128]{1,2,0:T(8,128)}, u32[]{:S(2)}) copy-start(f32[2,256,128]{1,2,0:T(8,128)} %reduce-scatter.5.cloned.1.call-done) | copy-start | bytes 786436
  258.9 109.0 %all-gather.7.cloned.1.call-start = ((), (), s32[]{:S(2)}) async-start(), calls=%async_computation.9 | async-start | bytes 1179648 | tf_op jit(solution)/shard_map/all_gather | solution.py:66
  328.7 76.5 %all-reduce.11.cloned.1.call-start = ((), (), s32[]{:S(2)}) async-start(), calls=%async_computation.10 | async-start | bytes 524288 | tf_op jit(solution)/shard_map/psum | solution.py:34
  367.9 2.7 copy-start.8
  373.7 104.7 %all-reduce.13.cloned.1.call-start = ((), (), s32[]{:S(2)}) async-start(), calls=%async_computation.11 | async-start | bytes 131072 | tf_op jit(solution)/shard_map/psum | solution.py:35
  407.3 158.5 %reduce-scatter.9.cloned.1.call-start = ((), (), s32[]{:S(2)}) async-start(), calls=%async_computation.12 | async-start | bytes 2359296 | tf_op jit(solution)/shard_map/reduce_scatter | solution.py:64
  487.4 4.5 copy-start.5
  491.9 2.8 copy-start.2
  496.7 110.0 %all-gather.9.cloned.1.call-start = ((), (), s32[]{:S(2)}) async-start(), calls=%async_computation.13 | async-start | bytes 1179648 | tf_op jit(solution)/shard_map/all_gather | solution.py:66
  567.5 116.0 %reduce-scatter.11.cloned.1.call-start = ((), (), s32[]{:S(2)}) async-start(), calls=%async_computation.14 | async-start | bytes 2359296 | tf_op jit(solution)/shard_map/reduce_scatter | solution.py:64
  615.4 68.1 %copy-start.7 = (f32[2,256,128]{1,2,0:T(8,128)S(1)}, f32[2,256,128]{1,2,0:T(8,128)}, u32[]{:S(2)}) copy-start(f32[2,256,128]{1,2,0:T(8,128)} %reduce-scatter.9.cloned.1.call-done) | copy-start | bytes 786436
  615.4 109.0 %all-gather.11.cloned.1.call-start = ((), (), s32[]{:S(2)}) async-start(), calls=%async_computation.15 | async-start | bytes 1179648 | tf_op jit(solution)/shard_map/all_gather | solution.py:66
  685.2 76.5 %all-reduce.15.cloned.1.call-start = ((), (), s32[]{:S(2)}) async-start(), calls=%async_computation.16 | async-start | bytes 524288 | tf_op jit(solution)/shard_map/psum | solution.py:34
  724.4 2.7 copy-start.9
  730.3 104.6 %all-reduce.17.cloned.1.call-start = ((), (), s32[]{:S(2)}) async-start(), calls=%async_computation.17 | async-start | bytes 131072 | tf_op jit(solution)/shard_map/psum | solution.py:35
  843.8 4.5 copy-start.3
Sparse Core Ops, SparseCore 0:
  13.0 35.0 all-reduce.6
  52.0 69.2 all-reduce.8
  139.7 68.8 reduce-scatter.4
  211.0 38.3 all-gather.4
  259.0 67.8 reduce-scatter.6
  329.4 38.4 all-gather.6
  373.9 31.2 all-reduce.10
  409.2 69.2 all-reduce.12
  496.8 68.9 reduce-scatter.8
  568.2 38.3 all-gather.8
  615.6 67.9 reduce-scatter.10
  686.0 38.3 all-gather.10
  730.4 31.2 all-reduce.14
  765.6 69.2 all-reduce.16
where the time goes:
time: 857 us; the launch traced here: 856 us
  waiting for transfers between devices  740 us (86%)
  matrix products  70.7 us (8%)
  other arithmetic  23.3 us (3%)
  between operations  19.3 us (2%)
    reduce_scatter x4, waiting for transfers between devices, body(): lax.psum_scatter(terms, 'samp', scatter_dimension=1, tiled=True)  273 us
    psum x3, waiting for transfers between devices, make_scores(): gram = lax.psum(jnp.dot(summed.T, summed, precision=HIGH), 'samp')  212 us
    all_gather x4, waiting for transfers between devices, body(): lax.all_gather(own_coeffs.astype(jnp.bfloat16), 'samp', axis=1, tiled=True)  157 us
    psum x3, waiting for transfers between devices, make_scores(): summed = lax.psum(local_sum, 'view')  97.5 us
    dot_general x8, matrix products, grad_term(): lax.dot_general(samples, resid, (((0,), (0,)), ((), ())), preferred_eleme...  20.6 us
  transfers between devices with their start and end apart: 14, of which 14 were waited for; matrix products, arithmetic and copies ran while one was open for 0% of the time, Pallas kernels for 0%

commit v1 on v0

--- a/solution.py
+++ b/solution.py
@@ -31,7 +31,9 @@
         local_sum = local_sum + jnp.dot(
             view_data[member], coeffs_low[member], preferred_element_type=jnp.float32
         )
-    summed = lax.psum(local_sum, "view")
+    summed = local_sum
+    for hop in (1, 2):
+        summed = summed + lax.ppermute(summed, "view", [(dev, dev ^ hop) for dev in range(4)])
     gram = lax.psum(jnp.dot(summed.T, summed, precision=HIGH), "samp")
     inverse, scale = newton_inverse(gram)
     return jnp.dot(summed, inverse, precision=HIGH) * jnp.sqrt(total / scale)

time: 857 us -> 781 us (0.911)
  waiting for transfers between devices: 740 us -> 661 us
    psum x3 -> x0, waiting for transfers between devices: 97.5 us -> none  [make_scores(): summed = lax.psum(local_sum, 'view')]
    ppermute x0 -> x6, waiting for transfers between devices: none -> 24.3 us  [make_scores(): lax.ppermute(summed, 'view', [(dev, dev ^ hop) for dev in range(4)])]
  transfers between devices with their start and end apart: 14 -> 17, of which waited for: 14 -> 17; matrix products, arithmetic and copies ran while one was open for 0% -> 0% of each run, Pallas kernels for 0% -> 0%
where the time goes in v1:
time: 781 us; the launch traced here: 780 us
  waiting for transfers between devices  661 us (85%)
  matrix products  65.4 us (8%)
  other arithmetic  23.5 us (3%)
  between operations  19.2 us (2%)
    reduce_scatter x4, waiting for transfers between devices, body(): lax.psum_scatter(terms, 'samp', scatter_dimension=1, tiled=True)  274 us
    psum x3, waiting for transfers between devices, make_scores(): gram = lax.psum(jnp.dot(summed.T, summed, precision=HIGH), 'samp')  207 us
    all_gather x4, waiting for transfers between devices, body(): lax.all_gather(own_coeffs.astype(jnp.bfloat16), 'samp', axis=1, tiled=True)  157 us
    ppermute x6, waiting for transfers between devices, make_scores(): lax.ppermute(summed, 'view', [(dev, dev ^ hop) for dev in range(4)])  24.3 us
    dot_general x8, matrix products, grad_term(): lax.dot_general(samples, resid, (((0,), (0,)), ((), ())), preferred_eleme...  20.6 us
  transfers between devices with their start and end apart: 17, of which 17 were waited for; matrix products, arithmetic and copies ran while one was open for 0% of the time, Pallas kernels for 0%

profile of v1, /device:TPU:0, one launch (start us, length us, event | category | flops | bytes accessed | tf_op | source)
XLA Modules:
  0.0 779.6 jit_solution(14524889822174105532)
XLA Ops:
  7.2 1.9 convert_element_type.42
  9.1 2.3 fusion.12
  11.4 0.7 fusion.163
  12.1 0.6 collective-permute-start
  12.7 1.2 collective-permute-done
  13.9 2.9 collective-permute-start.1
  16.8 6.6 collective-permute-done.1
  23.5 1.2 fusion.165
  24.7 70.9 %all-reduce.4.cloned.1.call-done = f32[128,128]{1,0:T(8,128)} async-done(((f32[128,128]{1,0:T(8,128)}), f32[128,128]{1,0:T(8,128)}) %all-reduce.4.cloned.1.call-update) | async-done | bytes 65552 | tf_op jit(solution)/shard_map/psum | solution.py:37
  95.6 1.5 select_reduce_fusion.2
  97.7 1.5 multiply_reduce_fusion.2
  99.9 1.0 fusion.119
  101.1 1.1 fusion.152
  109.0 0.4 convolution_multiply_fusion.2
  109.4 2.3 convolution_bitcast_fusion.6
  111.9 0.5 convolution_bitcast_fusion.7
  112.3 1.5 pad_maximum_fusion
  113.9 1.0 constant_dynamic-slice_fusion
  115.0 68.1 %reduce-scatter.5.cloned.1.call-done = f32[2,256,128]{1,2,0:T(8,128)} async-done(((f32[2,2048,128]{1,2,0:T(8,128)}), f32[2,256,128]{1,2,0:T(8,128)}) %reduce-scatter.5.cloned.1.call-update) | async-done | bytes 262160 | tf_op jit(solution)/shard_map/reduce_scatter | solution.py:66
  183.1 1.7 fusion.144
  184.8 39.4 %all-gather.5.cloned.1.call-done = bf16[2,2048,128]{1,2,0:T(8,128)(2,1)} async-done(((bf16[2,256,128]{1,2,0:T(8,128)(2,1)}), bf16[2,2048,128]{1,2,0:T(8,128)(2,1)}) %all-gather.5.cloned.1.call-update) | async-done | bytes 1048592 | tf_op jit(solution)/shard_map/all_gather | solution.py:68
  224.2 4.0 convolution_bitcast_fusion.4
  228.2 4.0 convolution_bitcast_fusion.5
  232.1 1.5 pad_maximum_fusion.1
  233.7 68.3 %reduce-scatter.7.cloned.1.call-done = f32[2,256,128]{1,2,0:T(8,128)} async-done(((f32[2,2048,128]{1,2,0:T(8,128)}), f32[2,256,128]{1,2,0:T(8,128)}) %reduce-scatter.7.cloned.1.call-update) | async-done | bytes 262160 | tf_op jit(solution)/shard_map/reduce_scatter | solution.py:66
  302.0 1.7 fusion.162
  303.9 38.9 %all-gather.7.cloned.1.call-done = bf16[2,2048,128]{1,2,0:T(8,128)(2,1)} async-done(((bf16[2,256,128]{1,2,0:T(8,128)(2,1)}), bf16[2,2048,128]{1,2,0:T(8,128)(2,1)}) %all-gather.7.cloned.1.call-update) | async-done | bytes 1048592 | tf_op jit(solution)/shard_map/all_gather | solution.py:68
  342.9 2.7 fusion.55
  345.6 2.4 fusion.164
  348.1 1.5 collective-permute-done.2
  349.6 1.7 collective-permute-start.3
  351.3 6.8 collective-permute-done.3
  358.1 1.0 fusion.187
  359.2 68.4 %all-reduce.6.cloned.1.call-done = f32[128,128]{1,0:T(8,128)} async-done(((f32[128,128]{1,0:T(8,128)}), f32[128,128]{1,0:T(8,128)}) %all-reduce.6.cloned.1.call-update) | async-done | bytes 65552 | tf_op jit(solution)/shard_map/psum | solution.py:37
  427.5 1.5 select_reduce_fusion.1
  429.6 1.5 multiply_reduce_fusion.1
  431.8 1.0 fusion.107
  433.1 1.1 fusion.149
  441.0 0.4 convolution_multiply_fusion.1
  441.4 2.3 convolution_bitcast_fusion.2
  443.8 0.4 convolution_bitcast_fusion.3
  444.2 1.5 pad_maximum_fusion.2
  445.8 68.8 %reduce-scatter.9.cloned.1.call-done = f32[2,256,128]{1,2,0:T(8,128)} async-done(((f32[2,2048,128]{1,2,0:T(8,128)}), f32[2,256,128]{1,2,0:T(8,128)}) %reduce-scatter.9.cloned.1.call-update) | async-done | bytes 262160 | tf_op jit(solution)/shard_map/reduce_scatter | solution.py:66
  514.6 1.7 fusion.145
  516.3 39.3 %all-gather.9.cloned.1.call-done = bf16[2,2048,128]{1,2,0:T(8,128)(2,1)} async-done(((bf16[2,256,128]{1,2,0:T(8,128)(2,1)}), bf16[2,2048,128]{1,2,0:T(8,128)(2,1)}) %all-gather.9.cloned.1.call-update) | async-done | bytes 1048592 | tf_op jit(solution)/shard_map/all_gather | solution.py:68
  555.7 3.6 convolution_bitcast_fusion
  559.3 3.6 convolution_bitcast_fusion.1
  562.9 1.5 pad_maximum_fusion.3
  564.4 68.4 %reduce-scatter.11.cloned.1.call-done = f32[2,256,128]{1,2,0:T(8,128)} async-done(((f32[2,2048,128]{1,2,0:T(8,128)}), f32[2,256,128]{1,2,0:T(8,128)}) %reduce-scatter.11.cloned.1.call-update) | async-done | bytes 262160 | tf_op jit(solution)/shard_map/reduce_scatter | solution.py:66
  632.8 1.7 fusion.161
  634.8 38.9 %all-gather.11.cloned.1.call-done = bf16[2,2048,128]{1,2,0:T(8,128)(2,1)} async-done(((bf16[2,256,128]{1,2,0:T(8,128)(2,1)}), bf16[2,2048,128]{1,2,0:T(8,128)(2,1)}) %all-gather.11.cloned.1.call-update) | async-done | bytes 1048592 | tf_op jit(solution)/shard_map/all_gather | solution.py:68
  673.7 2.7 fusion
  676.4 2.4 fusion.46
  678.9 1.5 collective-permute-done.4
  680.5 1.6 collective-permute-start.5
  682.1 6.8 collective-permute-done.5
  688.9 1.0 fusion.209
  690.0 0.8 copy.6
  690.8 67.6 %all-reduce.8.cloned.1.call-done = f32[128,128]{1,0:T(8,128)} async-done(((f32[128,128]{1,0:T(8,128)}), f32[128,128]{1,0:T(8,128)}) %all-reduce.8.cloned.1.call-update) | async-done | bytes 65552 | tf_op jit(solution)/shard_map/psum | solution.py:37
  758.4 1.5 select_reduce_fusion
  760.5 1.5 multiply_reduce_fusion
  762.7 1.0 fusion.95
  763.9 1.1 fusion.146
  771.8 1.3 convolution_multiply_fusion
  (144 shorter events, 22.0 us)
Async XLA Ops:
  7.2 88.4 %all-reduce.4.cloned.1.call-start = ((), (), s32[]{:S(2)}) async-start(), calls=%async_computation.4 | async-start | bytes 131072 | tf_op jit(solution)/shard_map/psum | solution.py:37
  7.2 4.2 copy-start
  12.1 1.7 collective-permute-start
  13.9 9.5 %collective-permute-start.1 = (f32[512,128]{1,0:T(8,128)S(1)}, f32[512,128]{1,0:T(8,128)S(1)}, u32[]{:S(2)}, u32[]{:S(2)}) collective-permute-start(f32[512,128]{1,0:T(8,128)S(1)} %add.70), channel_id=1, source_target_pairs={{0,16},{8,24},{16,0},{24,8},{1,17},{9,25},{17,1},{25,9},{2,18},{10... | collective-permute-start | bytes 786440 | tf_op jit(solution)/shard_map/ppermute | solution.py:36
  24.7 158.4 %reduce-scatter.5.cloned.1.call-start = ((), (), s32[]{:S(2)}) async-start(), calls=%async_computation.5 | async-start | bytes 2359296 | tf_op jit(solution)/shard_map/reduce_scatter | solution.py:66
  109.0 2.8 copy-start.1
  113.8 110.3 %all-gather.5.cloned.1.call-start = ((), (), s32[]{:S(2)}) async-start(), calls=%async_computation.6 | async-start | bytes 1179648 | tf_op jit(solution)/shard_map/all_gather | solution.py:68
  184.7 117.2 %reduce-scatter.7.cloned.1.call-start = ((), (), s32[]{:S(2)}) async-start(), calls=%async_computation.7 | async-start | bytes 2359296 | tf_op jit(solution)/shard_map/reduce_scatter | solution.py:66
  233.6 68.4 %copy-start.3 = (f32[2,256,128]{1,2,0:T(8,128)S(1)}, f32[2,256,128]{1,2,0:T(8,128)}, u32[]{:S(2)}) copy-start(f32[2,256,128]{1,2,0:T(8,128)} %reduce-scatter.5.cloned.1.call-done) | copy-start | bytes 786436
  233.6 109.2 %all-gather.7.cloned.1.call-start = ((), (), s32[]{:S(2)}) async-start(), calls=%async_computation.8 | async-start | bytes 1179648 | tf_op jit(solution)/shard_map/all_gather | solution.py:68
  303.7 123.8 %all-reduce.6.cloned.1.call-start = ((), (), s32[]{:S(2)}) async-start(), calls=%async_computation.9 | async-start | bytes 131072 | tf_op jit(solution)/shard_map/psum | solution.py:37
  342.9 2.7 copy-start.5
  348.0 1.6 collective-permute-start.2
  349.6 8.4 %collective-permute-start.3 = (f32[512,128]{0,1:T(8,128)S(1)}, f32[512,128]{0,1:T(8,128)S(1)}, u32[]{:S(2)}, u32[]{:S(2)}) collective-permute-start(f32[512,128]{0,1:T(8,128)S(1)} %add.76), channel_id=1, source_target_pairs={{0,16},{8,24},{16,0},{24,8},{1,17},{9,25},{17,1},{25,9},{2,18},{10... | collective-permute-start | bytes 786440 | tf_op jit(solution)/shard_map/ppermute | solution.py:36
  359.1 155.5 %reduce-scatter.9.cloned.1.call-start = ((), (), s32[]{:S(2)}) async-start(), calls=%async_computation.10 | async-start | bytes 2359296 | tf_op jit(solution)/shard_map/reduce_scatter | solution.py:66
  440.9 2.8 copy-start.2
  445.7 110.0 %all-gather.9.cloned.1.call-start = ((), (), s32[]{:S(2)}) async-start(), calls=%async_computation.11 | async-start | bytes 1179648 | tf_op jit(solution)/shard_map/all_gather | solution.py:68
  516.3 116.5 %reduce-scatter.11.cloned.1.call-start = ((), (), s32[]{:S(2)}) async-start(), calls=%async_computation.12 | async-start | bytes 2359296 | tf_op jit(solution)/shard_map/reduce_scatter | solution.py:66
  564.4 68.4 %copy-start.4 = (f32[2,256,128]{1,2,0:T(8,128)S(1)}, f32[2,256,128]{1,2,0:T(8,128)}, u32[]{:S(2)}) copy-start(f32[2,256,128]{1,2,0:T(8,128)} %reduce-scatter.9.cloned.1.call-done) | copy-start | bytes 786436
  564.4 109.3 %all-gather.11.cloned.1.call-start = ((), (), s32[]{:S(2)}) async-start(), calls=%async_computation.13 | async-start | bytes 1179648 | tf_op jit(solution)/shard_map/all_gather | solution.py:68
  634.5 123.8 %all-reduce.8.cloned.1.call-start = ((), (), s32[]{:S(2)}) async-start(), calls=%async_computation.14 | async-start | bytes 131072 | tf_op jit(solution)/shard_map/psum | solution.py:37
  673.7 2.7 copy-start.6
  678.8 1.6 collective-permute-start.4
  680.5 8.4 %collective-permute-start.5 = (f32[512,128]{0,1:T(8,128)S(1)}, f32[512,128]{0,1:T(8,128)S(1)}, u32[]{:S(2)}, u32[]{:S(2)}) collective-permute-start(f32[512,128]{0,1:T(8,128)S(1)} %add.83), channel_id=1, source_target_pairs={{0,16},{8,24},{16,0},{24,8},{1,17},{9,25},{17,1},{25,9},{2,18},{10... | collective-permute-start | bytes 786440 | tf_op jit(solution)/shard_map/ppermute | solution.py:36
Sparse Core Ops, SparseCore 0:
  24.8 70.7 all-reduce.3
  114.0 69.0 reduce-scatter.4
  185.7 38.4 all-gather.4
  233.7 68.1 reduce-scatter.6
  304.4 38.3 all-gather.6
  359.2 68.2 all-reduce.5
  445.8 68.7 reduce-scatter.8
  517.2 38.3 all-gather.8
  564.5 68.2 reduce-scatter.10
  635.3 38.3 all-gather.10
  690.1 68.2 all-reduce.7
